TPU v7x, 32 devices: a whole 2x2x4 slice. The times are simulated.
32 devices in a mesh: groups: 2 (over x), seq: 16 (over z, y, core).
Axes of the slice: x: 2, y: 2, z: 4, core: 2. Of those that a mesh axis runs over, the one named last changes fastest.
Arguments:
- cache_keys: bfloat16 [131072, 1024], P(('groups', 'seq')), parts along dimension 0, may hold values from -48 to 48
- cache_values: bfloat16 [131072, 1024], P(('groups', 'seq')), parts along dimension 0, may hold values from -6 to 6
- sketch_matrix: float32 [1024, 160], replicated, may hold values from -6 to 6
- queries: bfloat16 [6, 8192], P('groups'), parts along dimension 0, may hold values from -2000 to 2000
- fresh_keys: bfloat16 [6, 1024], P('groups'), parts along dimension 0, may hold values from -20 to 20
- fresh_values: bfloat16 [6, 1024], P('groups'), parts along dimension 0, may hold values from -6 to 6
- chosen: int32 [6, 8, 256], P('groups'), parts along dimension 0, may hold values from 0 to 8191, as said below
- shard_counts: int32 [6, 8, 16], P('groups'), parts along dimension 0, may hold values from 0 to 48, as said below
- outliers: int32 [64], P('groups'), parts along dimension 0, may hold values from 0 to 8191, as said below
Outputs:
- attended: bfloat16 [6, 8192], P('groups', 'seq'), parts along dimension 0
- key_factor: float32 [131072, 160], P(('groups', 'seq')), parts along dimension 0
There are 2 independent parts, one for each index of `groups`. A program takes and returns all parts, laid end to end along the dimension named above; an argument that names none is the same for every part. Nothing has to cross between parts.
Inputs may be any that keep to these rules, and one draw needn't show every extreme that they name: Each list chosen[t, g] holds distinct span numbers in ascending order, none of them an outlier span; shard s holds spans s * 512 to (s+1) * 512 - 1. shard_counts[t, g, s] is the number of entries of chosen[t, g] on shard s; they sum to 256; the most is 48, reached in every list. `outliers`: distinct span numbers in ascending order; at most 4 on one shard, reached on some shard.
All inputs are finite; a program needn't handle non-finite values.
Results may differ from a plain program's by a relative error of at most 0.0228.
Values may be sent and summed in bfloat16 or wider, within the bound.
A program may use at most 128 MiB of HBM per device.

v0:
```python
import jax
import jax.numpy as jnp
from jax import lax
from jax.sharding import PartitionSpec as P

KVH = 8
HD = 128
QH = 64
SPAN = 8
OMOST = 4


def merged_2(x, axis, combine):
    everything = jax.tree.map(lambda part: lax.all_gather(part, axis), x)
    leading = jax.tree.map(lambda part: part[0], everything)

    def step(k, so_far):
        return combine(so_far, jax.tree.map(lambda part: part[k], everything))

    return lax.fori_loop(1, lax.axis_size(axis), step, leading)


def rotate(vectors, positions):
    half_width = vectors.shape[-1] // 2
    exponents = jnp.arange(half_width, dtype=jnp.float32) * (2.0 / vectors.shape[-1])
    inverse_freq = jnp.exp(-jnp.log(jnp.float32(500000.0)) * exponents)
    angles = positions.astype(jnp.float32)[..., None] * inverse_freq
    cosine = jnp.cos(angles)
    sine = jnp.sin(angles)
    first_half = vectors[..., :half_width]
    second_half = vectors[..., half_width:]
    return jnp.concatenate(
        [first_half * cosine - second_half * sine, second_half * cosine + first_half * sine],
        axis=-1,
    )


def make_basis(sketch):
    small_gram = jnp.dot(sketch.T, sketch, precision=lax.Precision.HIGHEST)
    lower = jnp.linalg.cholesky(small_gram)
    solved = lax.linalg.triangular_solve(lower, sketch.T, left_side=True, lower=True)
    return solved.T.astype(jnp.bfloat16)


def softmax_part(query_rows, key_rows, value_rows, is_live):
    score_scale = 1.0 / jnp.sqrt(jnp.float32(query_rows.shape[-1]))
    scores = (
        jnp.einsum(
            "...qd,...ld->...ql",
            query_rows,
            key_rows.astype(jnp.float32),
            precision=lax.Precision.HIGHEST,
        )
        * score_scale
    )
    live_mask = is_live[..., None, :]
    scores = jnp.where(live_mask, scores, -1e30)
    run_max = jnp.max(scores, axis=-1)
    weights = jnp.exp(scores - run_max[..., None]) * live_mask
    run_sum = jnp.sum(weights, axis=-1)
    run_out = jnp.einsum(
        "...ql,...ld->...qd",
        weights,
        value_rows.astype(jnp.float32),
        precision=lax.Precision.HIGHEST,
    )
    return (run_max, run_sum, run_out)


def combine(earlier, later):
    joint_max = jnp.maximum(earlier[0], later[0])
    scale_early = jnp.exp(earlier[0] - joint_max)
    scale_late = jnp.exp(later[0] - joint_max)
    return (
        joint_max,
        earlier[1] * scale_early + later[1] * scale_late,
        earlier[2] * scale_early[..., None] + later[2] * scale_late[..., None],
    )


def on_device(
    cache_keys,
    cache_values,
    sketch_matrix,
    queries,
    fresh_keys,
    fresh_values,
    chosen,
    shard_counts,
    outliers,
):
    seq_len, feature_width = cache_keys.shape
    devices = lax.axis_size("seq")
    myself = lax.axis_index("seq")
    length = seq_len * devices
    steps = queries.shape[0]
    group_size = QH // KVH
    per_device = QH // devices
    contract = (((0,), (0,)), ((), ()))
    gram_share = (
        lax.psum_scatter(
            lax.dot_general(cache_keys, cache_keys, contract, preferred_element_type=jnp.float32),
            "seq",
            scatter_dimension=0,
            tiled=True,
        )
        / length
    )
    sketch_share = jnp.dot(gram_share, sketch_matrix, precision=lax.Precision.HIGHEST)
    sketch = lax.all_gather(sketch_share, "seq", axis=0, tiled=True)
    key_basis = make_basis(sketch)
    rank_width = key_basis.shape[1]
    key_factor = jnp.dot(cache_keys, key_basis, preferred_element_type=jnp.float32)
    spans_dev = seq_len // SPAN
    most_slots = 3 * chosen.shape[2] // devices
    preceding = jnp.cumsum(shard_counts, axis=2) - shard_counts
    list_start = lax.dynamic_index_in_dim(preceding, myself, 2, keepdims=False)
    own_count = lax.dynamic_index_in_dim(shard_counts, myself, 2, keepdims=False)
    padded_list = jnp.concatenate([chosen, jnp.zeros((steps, KVH, most_slots), jnp.int32)], axis=2)
    slot_ids = jnp.arange(most_slots, dtype=jnp.int32)
    picked = jnp.take_along_axis(padded_list, list_start[..., None] + slot_ids, axis=2)
    is_live = slot_ids < own_count[..., None]
    shard_base = myself * spans_dev
    local_span = jnp.clip(picked - shard_base, 0, spans_dev - 1)
    factor_spans = key_factor.reshape(spans_dev, SPAN, rank_width)[local_span]
    basis_heads = key_basis.reshape(KVH, HD, rank_width).astype(jnp.float32)
    rebuilt = jnp.einsum(
        "tgmcr,gdr->tgmcd", factor_spans, basis_heads, precision=lax.Precision.HIGHEST
    )
    token_pos = (local_span + shard_base)[..., None] * SPAN + jnp.arange(SPAN, dtype=jnp.int32)
    sel_keys = rotate(rebuilt, token_pos).astype(jnp.bfloat16)
    value_blocks = cache_values.reshape(spans_dev, SPAN, KVH, HD)
    head_ids = jnp.arange(KVH, dtype=jnp.int32)
    sel_values = value_blocks[local_span, :, head_ids[None, :, None], :]
    outlier_here = outliers // spans_dev == myself
    outlier_order = jnp.cumsum(outlier_here.astype(jnp.int32)) - 1
    slot_match = outlier_here[None, :] & (
        outlier_order[None, :] == jnp.arange(OMOST, dtype=jnp.int32)[:, None]
    )
    outlier_local = jnp.sum(jnp.where(slot_match, outliers[None, :] - shard_base, 0), axis=1)
    outlier_live = jnp.any(slot_match, axis=1)
    key_blocks = cache_keys.reshape(spans_dev, SPAN, KVH, HD)
    out_keys = key_blocks[outlier_local[None, :], :, head_ids[:, None], :]
    out_pos = (outlier_local + shard_base)[:, None] * SPAN + jnp.arange(SPAN, dtype=jnp.int32)
    out_keys = rotate(out_keys.astype(jnp.float32), out_pos).astype(jnp.bfloat16)
    out_values = value_blocks[outlier_local[None, :], :, head_ids[:, None], :]
    slot_total = most_slots + OMOST
    slot_keys = jnp.concatenate(
        [sel_keys, jnp.broadcast_to(out_keys[None], (steps, KVH, OMOST, SPAN, HD))], axis=2
    )
    slot_values = jnp.concatenate(
        [sel_values, jnp.broadcast_to(out_values[None], (steps, KVH, OMOST, SPAN, HD))], axis=2
    )
    slot_live = jnp.concatenate(
        [is_live, jnp.broadcast_to(outlier_live[None, None], (steps, KVH, OMOST))], axis=2
    )
    step_pos = length + jnp.arange(steps, dtype=jnp.int32)
    query_rows = rotate(queries.reshape(steps, QH, HD).astype(jnp.float32), step_pos[:, None])
    own_queries = lax.dynamic_slice_in_dim(query_rows, myself * per_device, per_device, 1)
    grouped = query_rows.reshape(steps, KVH, group_size, HD)
    flat_keys = slot_keys.reshape(steps, KVH, slot_total * SPAN, HD)
    flat_values = slot_values.reshape(steps, KVH, slot_total * SPAN, HD)
    token_live = jnp.repeat(slot_live, SPAN, axis=2)
    local_stats = softmax_part(grouped, flat_keys, flat_values, token_live)
    merged = merged_2(local_stats, "seq", combine)
    run_max = lax.dynamic_slice_in_dim(
        merged[0].reshape(steps, QH), myself * per_device, per_device, 1
    )
    run_sum = lax.dynamic_slice_in_dim(
        merged[1].reshape(steps, QH), myself * per_device, per_device, 1
    )
    run_out = lax.dynamic_slice_in_dim(
        merged[2].reshape(steps, QH, HD), myself * per_device, per_device, 1
    )
    own_head = myself * per_device // group_size
    new_keys = lax.dynamic_index_in_dim(
        fresh_keys.reshape(steps, KVH, HD), own_head, 1, keepdims=False
    )
    new_keys = rotate(new_keys.astype(jnp.float32), step_pos).astype(jnp.bfloat16)
    new_values = lax.dynamic_index_in_dim(
        fresh_values.reshape(steps, KVH, HD), own_head, 1, keepdims=False
    )
    score_scale = 1.0 / jnp.sqrt(jnp.float32(HD))
    new_scores = (
        jnp.einsum(
            "thd,sd->ths",
            own_queries,
            new_keys.astype(jnp.float32),
            precision=lax.Precision.HIGHEST,
        )
        * score_scale
    )
    causal = jnp.arange(steps)[None, :] <= jnp.arange(steps)[:, None]
    new_scores = jnp.where(causal[:, None, :], new_scores, -1e30)
    joint_max = jnp.maximum(run_max, jnp.max(new_scores, axis=-1))
    old_scale = jnp.exp(run_max - joint_max)
    new_weights = jnp.exp(new_scores - joint_max[..., None]) * causal[:, None, :]
    summed = run_out * old_scale[..., None] + jnp.einsum(
        "ths,sd->thd", new_weights, new_values.astype(jnp.float32), precision=lax.Precision.HIGHEST
    )
    totals = run_sum * old_scale + jnp.sum(new_weights, axis=-1)
    attended = (summed / totals[..., None]).reshape(steps, per_device * HD).astype(jnp.bfloat16)
    return (attended, key_factor)


def solution(mesh):
    in_specs = (
        P(("groups", "seq"), None),
        P(("groups", "seq"), None),
        P(),
        P("groups", None),
        P("groups", None),
        P("groups", None),
        P("groups", None, None),
        P("groups", None, None),
        P("groups"),
    )
    out_specs = (P("groups", "seq"), P(("groups", "seq"), None))
    return jax.shard_map(
        on_device, mesh=mesh, in_specs=in_specs, out_specs=out_specs, check_vma=False
    )
```

profile of v0, /device:TPU:0, one launch (start us, length us, event | category | flops | bytes accessed | tf_op | source)
XLA Modules:
  0.0 298.8 jit_solution(4955914066819933756)
XLA Ops:
  7.2 15.1 %fusion.89 = f32[1024,1024]{1,0:T(8,128)} fusion(bf16[4096,1024]{1,0:T(8,128)(2,1)} %param.11), kind=kOutput, calls=%fused_computation.175 | convolution fusion | flops 8589934592 | bytes 12582912 | tf_op jit(solution)/shard_map/dot_general | solution.py:102
  23.4 9.4 %gather_fusion.4 = s32[1152]{0:T(1024)S(1)} fusion(s32[3,8,304]{2,1,0:T(8,128)S(1)} %concatenate.47, s32[1152]{0:T(1024)S(1)} %reshape.400), kind=kCustom, calls=%fused_computation.4 | custom fusion | bytes 23040 | tf_op jit(solution)/shard_map/jit(take_along_axis)/gather | solution.py:121
  33.8 4.5 %gather_fusion.1 = bf16[32,8,128]{2,1,0:T(8,128)(2,1)S(1)} fusion(bf16[512,8,8,128]{3,1,2,0:T(8,128)(2,1)} %bitcast.140, s32[32]{0:T(128)S(1)} %reshape.382), kind=kCustom, calls=%fused_computation.1 | custom fusion | bytes 131328 | tf_op jit(solution)/shard_map/gather | solution.py:143
  39.7 5.1 %gather_fusion.3 = bf16[32,8,128]{2,1,0:T(8,128)(2,1)} fusion(bf16[512,8,8,128]{3,1,2,0:T(8,128)(2,1)} %bitcast.145, s32[32]{0:T(128)S(1)} %reshape.382), kind=kCustom, calls=%fused_computation.3 | custom fusion | bytes 131328 | tf_op jit(solution)/shard_map/gather | solution.py:146
  44.8 14.9 %gather_fusion.2 = bf16[1152,8,128]{2,1,0:T(8,128)(2,1)} fusion(bf16[512,8,8,128]{3,1,2,0:T(8,128)(2,1)} %bitcast.146, s32[1152]{0:T(1024)S(1)} %reshape.388), kind=kCustom, calls=%fused_computation.2 | custom fusion | bytes 4727808 | tf_op jit(solution)/shard_map/gather | solution.py:134
  63.1 35.0 %reduce-scatter.2.cloned.1.call-done = f32[64,1024]{1,0:T(8,128)} async-done(((f32[1024,1024]{1,0:T(8,128)}), f32[64,1024]{1,0:T(8,128)}) %reduce-scatter.2.cloned.1.call-update) | async-done | bytes 262160 | tf_op jit(solution)/shard_map/reduce_scatter | solution.py:101
  98.1 1.7 fusion.36
  99.8 22.3 %all_gather.21 = f32[1024,160]{1,0:T(8,128)S(1)} all-gather(f32[64,160]{1,0:T(8,128)S(1)} %fusion.36), channel_id=1, replica_groups=mesh['groups'=2,'seq'=16] {'seq'}, dimensions={0}, use_global_device_ids=true | all-gather | bytes 696320 | tf_op jit(solution)/shard_map/all_gather | solution.py:110
  122.1 1.9 fusion.90
  124.1 11.7 %cholesky.51 = f32[128,128]{1,0:T(8,128)S(1)} custom-call(f32[128,128]{1,0:T(8,128)S(1)} %cholesky.124), custom_call_target="Cholesky" | custom-call | tf_op jit(solution)/shard_map/jit(cholesky)/cholesky | solution.py:40
  135.9 9.8 %custom-call.14 = f32[1,128,128]{1,2,0:T(8,128)S(1)} custom-call(f32[1,128,128]{2,1,0:T(8,128)S(1)} %get-tuple-element.236), custom_call_target="InvertDiagBlocksLowerTriangular" | custom-call | tf_op jit(solution)/shard_map/jit(cholesky)/cholesky | solution.py:40
  146.0 2.9 cholesky.110
  151.7 19.9 %custom-call.15 = f32[2,128,128]{1,2,0:T(8,128)S(1)} custom-call(f32[2,128,128]{2,1,0:T(8,128)S(1)} %pad_maximum_fusion.3), custom_call_target="InvertDiagBlocksLowerTriangular" | custom-call | tf_op jit(solution)/shard_map/triangular_solve | solution.py:41
  173.9 6.3 %convolution_bitcast_fusion = f32[4096,160]{0,1:T(8,128)S(1)} fusion(bf16[4096,1024]{1,0:T(8,128)(2,1)} %param.11, bf16[32,1024]{1,0:T(8,128)(2,1)S(1)} %convolution_convert_fusion, bf16[128,1024]{1,0:T(8,128)(2,1)S(1)} %get-tuple-element.249), kind=kOutput, calls=%fused_computation.21 | convolution fusion | flops 1342832640 | bytes 11337728 | tf_op jit(solution)/shard_map/dot_general | solution.py:113
  181.0 3.3 %copy.41 = f32[4096,160]{1,0:T(8,128)} copy(f32[4096,160]{0,1:T(8,128)S(1)} %convolution_bitcast_fusion) | data formatting | bytes 5242880 | tf_op jit(solution)/shard_map/dot_general | solution.py:113
  184.4 1.8 copy.55
  186.1 10.0 %gather_fusion = f32[1152,8,160]{2,1,0:T(8,128)} fusion(f32[512,8,160]{2,1,0:T(8,128)} %bitcast.136, s32[2048]{0:T(1024)} %pad_clamp_fusion), kind=kCustom, calls=%fused_computation | custom fusion | bytes 11801088 | tf_op jit(solution)/shard_map/gather | solution.py:125
  196.1 11.9 %fusion.19 = f32[3,8,48,8,128]{4,2,3,0,1:T(8,128)S(1)} fusion(f32[3,8,48,8,160]{4,3,2,1,0:T(8,128)} %bitcast.137, bf16[8,128,160,1,1]{1,0,2,4,3:T(8,128)(2,1)} %bitcast.143), kind=kOutput, calls=%fused_computation.34 | convolution fusion | flops 2264924160 | bytes 10944512 | tf_op jit(solution)/shard_map/tgmcr,gdr->tgmcd/dot_general | solution.py:127
  208.1 19.4 %fusion.10 = (bf16[3,8,48,8,64]{4,2,3,0,1:T(8,128)(2,1)S(1)}, bf16[3,8,48,8,64]{4,2,3,0,1:T(8,128)(2,1)S(1)}) fusion(f32[3,8,48,8,128]{4,2,3,0,1:T(8,128)S(1)} %fusion.19, f32[64]{0:T(128)S(1)} %multiply_exponential_fusion, f32[3,8,48,8]{2,3,0,1:T(8,128)S(1)} %copy-done.3), kind=kLoop, calls=%fused_computation.23 | loop fusion | flops 5308416 | bytes 7115008 | tf_op jit(solution)/shard_map/convert.11
  227.6 1.4 pad_maximum_fusion
  229.1 3.0 fusion.87
  232.1 2.2 fusion.13
  234.9 19.2 %all-gather.1 = f32[48,8,8]{2,1,0:T(8,128)S(1)} all-gather(f32[3,8,8]{2,1,0:T(8,128)S(1)} %fusion.35), channel_id=3, replica_groups=mesh['groups'=2,'seq'=16] {'seq'}, dimensions={0}, use_global_device_ids=true | all-gather | bytes 13056 | tf_op jit(solution)/shard_map/all_gather | solution.py:14
  254.1 18.4 %all-gather = f32[48,8,8]{2,1,0:T(8,128)S(1)} all-gather(f32[3,8,8]{2,1,0:T(8,128)S(1)} %get-tuple-element.251), channel_id=2, replica_groups=mesh['groups'=2,'seq'=16] {'seq'}, dimensions={0}, use_global_device_ids=true | all-gather | bytes 13056 | tf_op jit(solution)/shard_map/all_gather | solution.py:14
  273.4 16.3 %while.21 = (s32[]{:T(128)}, f32[3,8,8]{2,1,0:T(8,128)S(1)}, f32[3,8,8]{2,1,0:T(8,128)S(1)}, f32[3,8,8,128]{3,2,1,0:T(8,128)S(1)}, f32[16,3,8,8]{3,2,1,0:T(8,128...) while((s32[]{:T(128)}, f32[3,8,8]{2,1,0:T(8,128)S(1)}, ...), condition=%wide.region_12.13_spmd, body=%wide.region_11.12_spmd.sunk | while | flops 74885 | bytes 302743 | solution.py:20
  273.4 1.0 fusion.104
  274.5 1.0 fusion.104
  275.6 1.0 fusion.104
  276.7 1.0 fusion.104
  279.9 1.0 fusion.104
  283.2 1.0 fusion.104
  286.5 1.0 fusion.104
  (131 shorter events, 23.8 us)
Async XLA Ops:
  7.2 90.9 %copy-start = (f32[1024,160]{0,1:T(8,128)S(1)}, f32[1024,160]{0,1:T(8,128)}, u32[]{:S(2)}) copy-start(f32[1024,160]{0,1:T(8,128)} %param.13) | copy-start | bytes 1966084
  7.2 15.3 %copy-start.7 = (s32[3,8,16]{2,1,0:T(8,128)S(1)}, s32[3,8,16]{2,1,0:T(8,128)}, u32[]{:S(2)}) copy-start(s32[3,8,16]{2,1,0:T(8,128)} %param.18) | copy-start | bytes 4612
  7.2 16.2 %copy-start.8 = (s32[3,8,256]{2,1,0:T(8,128)S(1)}, s32[3,8,256]{2,1,0:T(8,128)}, u32[]{:S(2)}) copy-start(s32[3,8,256]{2,1,0:T(8,128)} %param.17) | copy-start | bytes 73732
  7.2 90.9 %reduce-scatter.2.cloned.1.call-start = ((), (), s32[]{:S(2)}) async-start(), calls=%async_computation.1 | async-start | bytes 4456448 | tf_op jit(solution)/shard_map/reduce_scatter | solution.py:101
  22.4 250.1 %all-gather.5.cloned.1.call-start = ((), (), s32[]{:S(2)}) async-start(), calls=%async_computation.2 | async-start | bytes 1671168 | tf_op jit(solution)/shard_map/all_gather | solution.py:14
  23.4 9.9 %copy-start.11 = (s32[32]{0:T(128)S(1)}, s32[32]{0:T(128)}, u32[]{:S(2)}) copy-start(s32[32]{0:T(128)} %param.19) | copy-start | bytes 388
  23.4 15.4 %copy-start.6 = (bf16[3,8192]{1,0:T(4,128)(2,1)S(1)}, bf16[3,8192]{1,0:T(4,128)(2,1)}, u32[]{:S(2)}) copy-start(bf16[3,8192]{1,0:T(4,128)(2,1)} %param.14) | copy-start | bytes 147460
  180.2 15.9 %copy-start.1 = (f32[4096,160]{0,1:T(8,128)}, f32[4096,160]{0,1:T(8,128)S(1)}, u32[]{:S(2)}) copy-start(f32[4096,160]{0,1:T(8,128)S(1)} %convolution_bitcast_fusion) | copy-start | bytes 7864324
  196.1 12.0 %copy-start.3 = (f32[3,8,48,8]{2,3,0,1:T(8,128)S(1)}, f32[3,8,48,8]{2,3,0,1:T(8,128)}, u32[]{:S(2)}) copy-start(f32[3,8,48,8]{2,3,0,1:T(8,128)} %add_convert_fusion.1) | copy-start | bytes 110596
  227.6 4.5 %copy-start.4 = (bf16[32,8,128]{2,1,0:T(8,128)(2,1)S(1)}, bf16[32,8,128]{2,1,0:T(8,128)(2,1)}, u32[]{:S(2)}) copy-start(bf16[32,8,128]{2,1,0:T(8,128)(2,1)} %gather_fusion.3) | copy-start | bytes 196612
  227.6 4.5 %copy-start.2 = (bf16[1152,8,128]{2,1,0:T(8,128)(2,1)S(1)}, bf16[1152,8,128]{2,1,0:T(8,128)(2,1)}, u32[]{:S(2)}) copy-start(bf16[1152,8,128]{2,1,0:T(8,128)(2,1)} %gather_fusion.2) | copy-start | bytes 7077892
  227.6 4.5 %copy-start.5 = (f32[3,8,416]{2,1,0:T(8,128)S(1)}, f32[3,8,416]{2,1,0:T(8,128)}, u32[]{:S(2)}) copy-start(f32[3,8,416]{2,1,0:T(8,128)} %convert_element_type.103) | copy-start | bytes 119812
  229.0 5.3 %copy-start.9 = (bf16[3,64]{1,0:T(4,128)(2,1)S(1)}, bf16[3,64]{1,0:T(4,128)(2,1)}, u32[]{:S(2)}) copy-start(bf16[3,64]{1,0:T(4,128)(2,1)} %get-tuple-element.239) | copy-start | bytes 1156
  229.1 5.3 %copy-start.10 = (bf16[3,64]{1,0:T(4,128)(2,1)S(1)}, bf16[3,64]{1,0:T(4,128)(2,1)}, u32[]{:S(2)}) copy-start(bf16[3,64]{1,0:T(4,128)(2,1)} %get-tuple-element.240) | copy-start | bytes 1156
Sparse Core Ops, SparseCore 0:
  22.5 75.5 reduce-scatter.1
  234.4 37.8 all-gather.4
where the time goes:
time: 303 us; the launch traced here: 299 us
  other arithmetic  89.2 us (29%)
  blocking collectives  59.9 us (20%)
  local copies, waits for them, and re-layouts  52.1 us (17%)
  matrix products  46 us (15%)
  waiting for transfers between devices  35 us (12%)
  between operations  16.1 us (5%)
    all_gather x2, blocking collectives, merged_2(): everything = jax.tree.map(lambda part: lax.all_gather(part, axis), x)  37.6 us
    reduce_scatter x1, waiting for transfers between devices, on_device(): lax.psum_scatter(lax.dot_general(cache_keys, cache_keys, contract, prefer...  35 us
    another operation x7, other arithmetic, make_basis(): lower = jnp.linalg.cholesky(small_gram)  25.8 us
    all_gather x1, blocking collectives, on_device(): sketch = lax.all_gather(sketch_share, 'seq', axis=0, tiled=True)  22.3 us
    another operation x5, other arithmetic  20.3 us
    another operation x6, other arithmetic, make_basis(): lax.linalg.triangular_solve(lower, sketch.T, left_side=True, lower=True)  20 us
    add x15, other arithmetic, combine(): earlier[2] * scale_early[..., None] + later[2] * scale_late[..., None]  15.6 us
    dot_general x1, matrix products, on_device(): lax.dot_general(cache_keys, cache_keys, contract, preferred_element_type=...  15.1 us
  transfers between devices with their start and end apart: 2, of which 1 were waited for; matrix products, arithmetic and copies ran while one was open for 14% of the time, Pallas kernels for 0%

commit v1 on v0

--- a/solution.py
+++ b/solution.py
@@ -2,6 +2,7 @@
 import jax.numpy as jnp
 from jax import lax
 from jax.sharding import PartitionSpec as P
+from jax.lax import axis_index, axis_size, ppermute
 
 KVH = 8
 HD = 128
@@ -107,7 +108,24 @@
         / length
     )
     sketch_share = jnp.dot(gram_share, sketch_matrix, precision=lax.Precision.HIGHEST)
-    sketch = lax.all_gather(sketch_share, "seq", axis=0, tiled=True)
+    raw_out = axis_size("seq")
+    current_block = axis_index("seq")
+    shaped, known, block_out = (raw_out, current_block, sketch_share.shape[0])
+    block_now, piece_out = (sketch_share, 1)
+    while piece_out < shaped:
+        block_now = jnp.concatenate(
+            [
+                block_now,
+                ppermute(
+                    block_now,
+                    "seq",
+                    perm=tuple(((j, (j - piece_out) % shaped) for j in range(shaped))),
+                ),
+            ],
+            0,
+        )
+        piece_out = 2 * piece_out
+    sketch = jnp.roll(block_now, known * block_out, 0)
     key_basis = make_basis(sketch)
     rank_width = key_basis.shape[1]
     key_factor = jnp.dot(cache_keys, key_basis, preferred_element_type=jnp.float32)

time: 303 us -> 347 us (1.15)
  waiting for transfers between devices: 35 us -> 87.3 us
  blocking collectives: 59.9 us -> 40 us
  local copies, waits for them, and re-layouts: 52.1 us -> 56.5 us
  starting transfers between devices: 0.08 us -> 4.45 us
    ppermute x0 -> x4, waiting for transfers between devices: none -> 31.1 us  [on_device(): ppermute(block_now, 'seq', perm=tuple(((j, (j - piece_out) % shaped) for...]
    all_gather x1 -> x0, blocking collectives: 22.3 us -> none  [on_device(): sketch = lax.all_gather(sketch_share, 'seq', axis=0, tiled=True)]
    reduce_scatter x1, waiting for transfers between devices: 35 us -> 56.2 us  [on_device(): lax.psum_scatter(lax.dot_general(cache_keys, cache_keys, contract, prefer...]
    ppermute x0 -> x4, starting transfers between devices: none -> 4.37 us  [on_device(): ppermute(block_now, 'seq', perm=tuple(((j, (j - piece_out) % shaped) for...]
  transfers between devices with their start and end apart: 2 -> 6, of which waited for: 1 -> 4; matrix products, arithmetic and copies ran while one was open for 14% -> 13% of each run, Pallas kernels for 0% -> 0%
where the time goes in v1:
time: 347 us; the launch traced here: 341 us
  other arithmetic  91.2 us (26%)
  waiting for transfers between devices  87.3 us (25%)
  local copies, waits for them, and re-layouts  56.5 us (16%)
  matrix products  45.2 us (13%)
  blocking collectives  40 us (12%)
  between operations  16.2 us (5%)
  starting transfers between devices  4.45 us (1%)
    reduce_scatter x1, waiting for transfers between devices, on_device(): lax.psum_scatter(lax.dot_general(cache_keys, cache_keys, contract, prefer...  56.2 us
    all_gather x2, blocking collectives, merged_2(): everything = jax.tree.map(lambda part: lax.all_gather(part, axis), x)  40 us
    ppermute x4, waiting for transfers between devices, on_device(): ppermute(block_now, 'seq', perm=tuple(((j, (j - piece_out) % shaped) for...  31.1 us
    another operation x7, other arithmetic, make_basis(): lower = jnp.linalg.cholesky(small_gram)  25.8 us
    another operation x6, other arithmetic, make_basis(): lax.linalg.triangular_solve(lower, sketch.T, left_side=True, lower=True)  21.3 us
    another operation x5, other arithmetic  20.3 us
    add x15, other arithmetic, combine(): earlier[2] * scale_early[..., None] + later[2] * scale_late[..., None]  15.6 us
    dot_general x1, matrix products, on_device(): lax.dot_general(cache_keys, cache_keys, contract, preferred_element_type=...  15.1 us
  transfers between devices with their start and end apart: 6, of which 4 were waited for; matrix products, arithmetic and copies ran while one was open for 13% of the time, Pallas kernels for 0%

profile of v1, /device:TPU:0, one launch (start us, length us, event | category | flops | bytes accessed | tf_op | source)
XLA Modules:
  0.0 341.3 jit_solution(9279495782561762764)
XLA Ops:
  7.2 15.1 %fusion.93 = f32[1024,1024]{1,0:T(8,128)} fusion(bf16[4096,1024]{1,0:T(8,128)(2,1)} %param.11), kind=kOutput, calls=%fused_computation.193 | convolution fusion | flops 8589934592 | bytes 12582912 | tf_op jit(solution)/shard_map/dot_general | solution.py:103
  24.0 9.0 %gather_fusion.4 = s32[1152]{0:T(1024)S(1)} fusion(s32[3,8,304]{2,1,0:T(8,128)S(1)} %concatenate.69, s32[1152]{0:T(1024)S(1)} %reshape.400), kind=kCustom, calls=%fused_computation.4 | custom fusion | bytes 23040 | tf_op jit(solution)/shard_map/jit(take_along_axis)/gather | solution.py:139
  33.7 4.5 %gather_fusion.1 = bf16[32,8,128]{2,1,0:T(8,128)(2,1)S(1)} fusion(bf16[512,8,8,128]{3,1,2,0:T(8,128)(2,1)} %bitcast.136, s32[32]{0:T(128)S(1)} %reshape.382), kind=kCustom, calls=%fused_computation.1 | custom fusion | bytes 131328 | tf_op jit(solution)/shard_map/gather | solution.py:161
  41.8 56.2 %reduce-scatter.2.cloned.1.call-done = f32[64,1024]{1,0:T(8,128)} async-done(((f32[1024,1024]{1,0:T(8,128)}), f32[64,1024]{1,0:T(8,128)}) %reduce-scatter.2.cloned.1.call-update) | async-done | bytes 262160 | tf_op jit(solution)/shard_map/reduce_scatter | solution.py:102
  98.0 1.7 constant_dynamic-update-slice_fusion.9
  100.0 1.7 collective-permute-done
  101.7 2.0 collective-permute-start.1
  104.4 3.5 %collective-permute-done.1 = f32[128,160]{1,0:T(8,128)S(1)} collective-permute-done((f32[128,160]{1,0:T(8,128)S(1)}, f32[128,160]{1,0:T(8,128)S(1)}, u32[]{:S(2)}, u32[]{:S(2)}) %collective-permute-start.1) | collective-permute-done | bytes 81952 | tf_op jit(solution)/shard_map/ppermute | solution.py:119
  108.6 2.0 collective-permute-start.2
  112.7 1.2 broadcast_in_dim.58
  114.7 4.6 %gather_fusion.3 = bf16[32,8,128]{2,1,0:T(8,128)(2,1)} fusion(bf16[512,8,8,128]{3,1,2,0:T(8,128)(2,1)} %bitcast.141, s32[32]{0:T(128)S(1)} %reshape.382), kind=kCustom, calls=%fused_computation.3 | custom fusion | bytes 131328 | tf_op jit(solution)/shard_map/gather | solution.py:164
  119.4 14.9 %gather_fusion.2 = bf16[1152,8,128]{2,1,0:T(8,128)(2,1)} fusion(bf16[512,8,8,128]{3,1,2,0:T(8,128)(2,1)} %bitcast.142, s32[1152]{0:T(1024)S(1)} %reshape.388), kind=kCustom, calls=%fused_computation.2 | custom fusion | bytes 4727808 | tf_op jit(solution)/shard_map/gather | solution.py:152
  135.9 25.8 %collective-permute-done.3 = f32[512,160]{1,0:T(8,128)S(1)} collective-permute-done((f32[512,160]{1,0:T(8,128)S(1)}, f32[512,160]{1,0:T(8,128)S(1)}, u32[]{:S(2)}, u32[]{:S(2)}) %collective-permute-start.3) | collective-permute-done | bytes 327712 | tf_op jit(solution)/shard_map/ppermute | solution.py:119
  161.9 1.3 copy-done.3
  163.2 2.1 fusion.32
  165.3 1.3 dynamic-slice_bitcast_fusion
  166.7 11.7 %cholesky.51 = f32[128,128]{1,0:T(8,128)S(1)} custom-call(f32[128,128]{1,0:T(8,128)S(1)} %cholesky.124), custom_call_target="Cholesky" | custom-call | tf_op jit(solution)/shard_map/jit(cholesky)/cholesky | solution.py:41
  178.5 9.8 %custom-call.14 = f32[1,128,128]{1,2,0:T(8,128)S(1)} custom-call(f32[1,128,128]{2,1,0:T(8,128)S(1)} %get-tuple-element.236), custom_call_target="InvertDiagBlocksLowerTriangular" | custom-call | tf_op jit(solution)/shard_map/jit(cholesky)/cholesky | solution.py:41
  188.6 2.9 cholesky.110
  194.4 19.9 %custom-call.15 = f32[2,128,128]{1,2,0:T(8,128)S(1)} custom-call(f32[2,128,128]{2,1,0:T(8,128)S(1)} %pad_maximum_fusion.6), custom_call_target="InvertDiagBlocksLowerTriangular" | custom-call | tf_op jit(solution)/shard_map/triangular_solve | solution.py:42
  216.6 6.3 %convolution_bitcast_fusion = f32[4096,160]{0,1:T(8,128)S(1)} fusion(bf16[4096,1024]{1,0:T(8,128)(2,1)} %param.11, bf16[32,1024]{1,0:T(8,128)(2,1)S(1)} %convolution_convert_fusion, bf16[128,1024]{1,0:T(8,128)(2,1)S(1)} %get-tuple-element.251), kind=kOutput, calls=%fused_computation.21 | convolution fusion | flops 1342832640 | bytes 11337728 | tf_op jit(solution)/shard_map/dot_general | solution.py:131
  223.8 3.3 copy.41
  227.1 9.9 %gather_fusion = f32[1152,8,160]{2,1,0:T(8,128)} fusion(f32[512,8,160]{2,1,0:T(8,128)} %bitcast.134, s32[2048]{0:T(1024)S(1)} %copy-done.12), kind=kCustom, calls=%fused_computation | custom fusion | bytes 11801088 | tf_op jit(solution)/shard_map/gather | solution.py:143
  237.0 11.0 %fusion.19 = f32[3,8,48,8,128]{4,2,3,0,1:T(8,128)S(1)} fusion(f32[3,8,48,8,160]{4,3,2,1,0:T(8,128)} %bitcast.135, bf16[8,128,160,1,1]{1,0,2,4,3:T(8,128)(2,1)S(1)} %bitcast.139), kind=kOutput, calls=%fused_computation.34 | convolution fusion | flops 2264924160 | bytes 10944512 | tf_op jit(solution)/shard_map/tgmcr,gdr->tgmcd/dot_general | solution.py:145
  248.1 19.4 %fusion.10 = (bf16[3,8,48,8,64]{4,2,3,0,1:T(8,128)(2,1)S(1)}, bf16[3,8,48,8,64]{4,2,3,0,1:T(8,128)(2,1)S(1)}) fusion(f32[3,8,48,8,128]{4,2,3,0,1:T(8,128)S(1)} %fusion.19, f32[64]{0:T(128)S(1)} %copy-done.16, f32[3,8,48,8]{2,3,0,1:T(8,128)S(1)} %copy-done.5), kind=kLoop, calls=%fused_computation.23 | loop fusion | flops 5308416 | bytes 7115008 | tf_op jit(solution)/shard_map/convert.11
  267.6 1.4 pad_maximum_fusion
  269.1 3.0 fusion.91
  272.2 2.2 fusion.13
  274.9 21.6 %all-gather.1 = f32[48,8,8]{2,1,0:T(8,128)S(1)} all-gather(f32[3,8,8]{2,1,0:T(8,128)S(1)} %fusion.37), channel_id=3, replica_groups=mesh['groups'=2,'seq'=16] {'seq'}, dimensions={0}, use_global_device_ids=true | all-gather | bytes 13056 | tf_op jit(solution)/shard_map/all_gather | solution.py:15
  296.6 18.4 %all-gather = f32[48,8,8]{2,1,0:T(8,128)S(1)} all-gather(f32[3,8,8]{2,1,0:T(8,128)S(1)} %get-tuple-element.253), channel_id=2, replica_groups=mesh['groups'=2,'seq'=16] {'seq'}, dimensions={0}, use_global_device_ids=true | all-gather | bytes 13056 | tf_op jit(solution)/shard_map/all_gather | solution.py:15
  315.9 16.3 %while.21 = (s32[]{:T(128)}, f32[3,8,8]{2,1,0:T(8,128)S(1)}, f32[3,8,8]{2,1,0:T(8,128)S(1)}, f32[3,8,8,128]{3,2,1,0:T(8,128)S(1)}, f32[16,3,8,8]{3,2,1,0:T(8,128...) while((s32[]{:T(128)}, f32[3,8,8]{2,1,0:T(8,128)S(1)}, ...), condition=%wide.region_12.13_spmd, body=%wide.region_11.12_spmd.sunk | while | flops 74885 | bytes 302743 | solution.py:21
  318.1 1.0 fusion.104
  (167 shorter events, 35.8 us)
Async XLA Ops:
  7.2 90.8 %copy-start = (f32[1024,160]{0,1:T(8,128)S(1)}, f32[1024,160]{0,1:T(8,128)}, u32[]{:S(2)}) copy-start(f32[1024,160]{0,1:T(8,128)} %param.13) | copy-start | bytes 1966084
  7.2 90.8 %reduce-scatter.2.cloned.1.call-start = ((), (), s32[]{:S(2)}) async-start(), calls=%async_computation.1 | async-start | bytes 4456448 | tf_op jit(solution)/shard_map/reduce_scatter | solution.py:102
  22.3 0.7 copy-start.13
  22.3 1.6 copy-start.14
  22.4 292.6 %all-gather.5.cloned.1.call-start = ((), (), s32[]{:S(2)}) async-start(), calls=%async_computation.2 | async-start | bytes 1671168 | tf_op jit(solution)/shard_map/all_gather | solution.py:15
  24.0 9.3 %copy-start.19 = (s32[32]{0:T(128)S(1)}, s32[32]{0:T(128)}, u32[]{:S(2)}) copy-start(s32[32]{0:T(128)} %param.19) | copy-start | bytes 388
  24.0 14.2 %copy-start.11 = (bf16[3,8192]{1,0:T(4,128)(2,1)S(1)}, bf16[3,8192]{1,0:T(4,128)(2,1)}, u32[]{:S(2)}) copy-start(bf16[3,8192]{1,0:T(4,128)(2,1)} %param.14) | copy-start | bytes 147460
  38.5 3.3 copy-start.15
  99.7 2.0 collective-permute-start
  101.7 6.1 %collective-permute-start.1 = (f32[128,160]{1,0:T(8,128)S(1)}, f32[128,160]{1,0:T(8,128)S(1)}, u32[]{:S(2)}, u32[]{:S(2)}) collective-permute-start(f32[128,160]{1,0:T(8,128)S(1)} %pad_maximum_fusion.5), channel_id=1, source_target_pairs={{0,14},{1,15},{2,0},{3,1},{4,2},{5,3},{6,4},{7,5},{8,6},{9,7},{10,... | collective-permute-start | bytes 245768 | tf_op jit(solution)/shard_map/ppermute | solution.py:119
  108.6 27.0 %collective-permute-start.2 = (f32[256,160]{1,0:T(8,128)}, f32[256,160]{1,0:T(8,128)S(1)}, u32[]{:S(2)}, u32[]{:S(2)}) collective-permute-start(f32[256,160]{1,0:T(8,128)} %pad_maximum_fusion.3), channel_id=1, source_target_pairs={{0,12},{1,13},{2,14},{3,15},{4,0},{5,1},{6,2},{7,3},{8,4},{9,5},{1... | collective-permute-start | bytes 491528 | tf_op jit(solution)/shard_map/ppermute | solution.py:119
  113.9 20.3 %copy-start.9 = (pred[3,8,416]{2,1,0:T(8,128)(4,1)}, pred[3,8,416]{2,1,0:T(8,128)(4,1)S(1)}, u32[]{:S(2)}) copy-start(pred[3,8,416]{2,1,0:T(8,128)(4,1)S(1)} %broadcast_in_dim.58) | copy-start | bytes 29956
  135.6 26.1 %collective-permute-start.3 = (f32[512,160]{1,0:T(8,128)S(1)}, f32[512,160]{1,0:T(8,128)S(1)}, u32[]{:S(2)}, u32[]{:S(2)}) collective-permute-start(f32[512,160]{1,0:T(8,128)S(1)} %pad_maximum_fusion.1), channel_id=1, source_target_pairs={{0,8},{1,9},{2,10},{3,11},{4,12},{5,13},{6,14},{7,15},{8,0},{9,1},... | collective-permute-start | bytes 983048 | tf_op jit(solution)/shard_map/ppermute | solution.py:119
  161.9 1.3 copy-start.3
  222.9 4.2 %copy-start.1 = (f32[4096,160]{0,1:T(8,128)}, f32[4096,160]{0,1:T(8,128)S(1)}, u32[]{:S(2)}) copy-start(f32[4096,160]{0,1:T(8,128)S(1)} %convolution_bitcast_fusion) | copy-start | bytes 7864324
  223.8 3.4 copy-start.12
  227.1 9.9 %copy-start.4 = (bf16[20,8,8,128]{3,2,1,0:T(8,128)(2,1)S(1)}, bf16[20,8,8,128]{3,2,1,0:T(8,128)(2,1)}, u32[]{:S(2)}) copy-start(bf16[20,8,8,128]{3,2,1,0:T(8,128)(2,1)} %copy.55) | copy-start | bytes 983044
  237.0 11.0 %copy-start.5 = (f32[3,8,48,8]{2,3,0,1:T(8,128)S(1)}, f32[3,8,48,8]{2,3,0,1:T(8,128)}, u32[]{:S(2)}) copy-start(f32[3,8,48,8]{2,3,0,1:T(8,128)} %add_convert_fusion.1) | copy-start | bytes 110596
  237.0 11.0 %copy-start.16 = (f32[64]{0:T(128)S(1)}, f32[64]{0:T(128)}, u32[]{:S(2)}) copy-start(f32[64]{0:T(128)} %copy-done.15) | copy-start | bytes 772
  248.1 19.5 %copy-start.7 = (bf16[8,4,8,128]{3,1,2,0:T(4,128)(2,1)S(1)}, bf16[8,4,8,128]{3,1,2,0:T(4,128)(2,1)}, u32[]{:S(2)}) copy-start(bf16[8,4,8,128]{3,1,2,0:T(4,128)(2,1)} %copy.45) | copy-start | bytes 196612
  267.6 1.5 copy-start.10
  269.1 3.0 copy-start.6
  269.1 3.1 copy-start.2
  269.1 3.1 copy-start.8
  272.1 2.3 copy-start.17
  272.1 2.3 copy-start.18
Sparse Core Ops, SparseCore 0:
  22.5 75.4 reduce-scatter.1
  274.5 40.2 all-gather.4
